TPU v7x, 32 devices: a whole 2x2x4 slice. The times are simulated.
32 devices in a mesh: space: 4 (over y, core), mode: 8 (over z, x).
Axes of the slice: x: 2, y: 2, z: 4, core: 2. Of those that a mesh axis runs over, the one named last changes fastest.
Arguments:
- intensity: float32 [1024, 8, 64, 256], P('mode', None, 'space'), may hold values from 0.1 to 2
- dir_cos: float32 [3, 32], replicated, may hold values from -1 to 1, as said below
- velocity: float32 [32], replicated, may hold values from 0.2 to 1
- rate: float32 [32], replicated, may hold values from 0.05 to 2
- spectrum: float32 [32], replicated, may hold values from 0.2 to 2
- weight: float32 [32], replicated, may hold values from 0.25 to 1.75
- heat: float32 [64, 256], P('space'), may hold values from 0.5 to 4
- rough_cells: int32 [4096], P('space'), may hold values from 0 to 4095, as said below
- rough_count: int32 [4], P('space'), may hold values from 256 to 1024, as said below
- rough_map: int32 [4096, 16], P('space'), may hold values from 0 to 15
Outputs:
- intensity_new: float32 [1024, 8, 64, 256], P('mode', None, 'space')
- energy_new: float32 [8, 64, 256], P(None, 'space')
Inputs may be any that keep to these rules, and one draw needn't show every extreme that they name: `dir_cos`: even directions have a positive third cosine, and direction 2k+1 equals direction 2k with the third cosine negated; every direction has a third cosine of magnitude 0.3 or more. `rough_cells`: the entries of one index of space are distinct. `rough_count`: some index of space has all 1024 slots live.
All inputs are finite; a program needn't handle non-finite values.
Results may differ from a plain program's by a relative error of at most 0.0015.
Values sent between devices are 32-bit elements; how exact they have to be, the bound alone decides.
A program may use at most 128 MiB of HBM per device.

v0:
```python
import jax
import jax.numpy as jnp
from jax import lax
from jax.sharding import PartitionSpec as P

PAIRS = 1024


def extended(block, sides, width):
    for axis, dim in sides:
        count = lax.axis_size(axis)
        forward = [(i, i + 1) for i in range(count - 1)]
        backward = [(target, source) for source, target in forward]
        low = lax.ppermute(
            lax.slice_in_dim(block, block.shape[dim] - width, None, axis=dim), axis, forward
        )
        high = lax.ppermute(lax.slice_in_dim(block, 0, width, axis=dim), axis, backward)
        block = jnp.concatenate([low, block, high], axis=dim)
    return block


def squash(energy):
    return energy / (1.0 + 0.3 * jnp.abs(energy))


def per_device(
    intensity, dir_cos, velocity, rate, spectrum, weight, heat, rough_cells, rough_count, rough_map
):
    pairs_local = intensity.shape[0]
    modes = velocity.shape[0]
    planes_count, rows, width = (intensity.shape[1], intensity.shape[2], intensity.shape[3])
    dirs_local = pairs_local // modes
    half = dirs_local // 2
    position = lax.axis_index("mode")
    cos_local = lax.dynamic_slice_in_dim(dir_cos, position * dirs_local, dirs_local, 1)
    weight_local = lax.dynamic_slice_in_dim(weight, position * dirs_local, dirs_local, 0)
    field = intensity.reshape(dirs_local, modes, planes_count, rows, width)
    partial_value = jnp.einsum("s,smzxy->zxy", weight_local, field)
    energy = lax.psum(partial_value, "mode") / PAIRS
    equil = squash(energy)
    padded = extended(field, (("space", 3),), 1)
    ox = cos_local[0][:, None, None, None, None]
    oy = cos_local[1][:, None, None, None, None]
    speed = velocity[None, :, None, None, None]
    pady = jnp.pad(field, ((0, 0), (0, 0), (0, 0), (0, 0), (1, 1)))
    along = jnp.maximum(ox, 0.0) * (field - padded[:, :, :, :-2]) + jnp.minimum(ox, 0.0) * (
        padded[:, :, :, 2:] - field
    )
    across = jnp.maximum(oy, 0.0) * (field - pady[..., :-2]) + jnp.minimum(oy, 0.0) * (
        pady[..., 2:] - field
    )
    source = (rate * spectrum)[:, None, None, None] * equil[None]
    rhs = field + source[None] - speed * (along + across)
    diag = 1.0 + rate
    couple = velocity[None, :] * jnp.abs(cos_local[2])[:, None]
    cdown = couple[1::2][:, :, None, None]
    adown = diag[None, :, None, None] + cdown
    down_rhs = rhs[1::2]
    carry = spectrum[None, :, None, None] * heat[None, None]
    planes = [None] * planes_count
    for level in reversed(range(planes_count)):
        carry = (down_rhs[:, :, level] + cdown * carry) / adown
        planes[level] = carry
    down_new = jnp.stack(planes, axis=2)
    bottom = down_new[:, :, 0].reshape(half, modes, rows * width)
    slots = rough_cells.shape[0]
    live = jnp.arange(slots, dtype=jnp.int32) < rough_count[0]
    everything = lax.all_gather(bottom, "mode", axis=0, tiled=True)
    values = everything[:, :, rough_cells]
    targets = lax.dynamic_slice_in_dim(rough_map, position * half, half, 1)
    picked = jnp.take_along_axis(values.transpose(2, 0, 1), targets[:, :, None], axis=1).transpose(
        1, 2, 0
    )
    current = bottom[:, :, rough_cells]
    inflow = 0.9 * bottom.at[:, :, rough_cells].set(jnp.where(live[None, None, :], picked, current))
    carry = inflow.reshape(half, modes, rows, width)
    cup = couple[0::2][:, :, None, None]
    aup = diag[None, :, None, None] + cup
    up_rhs = rhs[0::2]
    planes = []
    for level in range(planes_count):
        carry = (up_rhs[:, :, level] + cup * carry) / aup
        planes.append(carry)
    up_new = jnp.stack(planes, axis=2)
    fresh = jnp.stack([up_new, down_new], axis=1).reshape(
        dirs_local, modes, planes_count, rows, width
    )
    energy_new = lax.psum(jnp.einsum("s,smzxy->zxy", weight_local, fresh), "mode") / PAIRS
    return (fresh.reshape(pairs_local, planes_count, rows, width), energy_new)


def solution(mesh):
    in_specs = (
        P("mode", None, "space", None),
        P(),
        P(),
        P(),
        P(),
        P(),
        P("space", None),
        P("space"),
        P("space"),
        P("space", None),
    )
    out_specs = (P("mode", None, "space", None), P(None, "space", None))
    return jax.shard_map(
        per_device, mesh=mesh, in_specs=in_specs, out_specs=out_specs, check_vma=False
    )
```

profile of v0, /device:TPU:0, one launch (start us, length us, event | category | flops | bytes accessed | tf_op | source)
XLA Modules:
  0.0 554.7 jit_solution(16689023233069573652)
XLA Ops:
  7.2 7.9 %bitcast_reduce_fusion = bf16[4,8,16,256]{3,2,1,0:T(8,128)(2,1)S(1)} fusion(f32[128,8,16,256]{3,2,1,0:T(8,128)} %param.10), kind=kLoop, calls=%fused_computation.96 | loop fusion | flops 4063232 | bytes 17039360 | tf_op jit(solution)/shard_map/s,smzxy->zxy/reduce_sum | solution.py:38
  16.3 8.0 %fusion.37 = (f32[4,32,8,1,256]{4,3,2,1,0:T(1,128)S(1)}, f32[4,32,8,1,256]{4,3,2,1,0:T(1,128)S(1)}) fusion(f32[4,32,8,16,256]{4,3,2,1,0:T(8,128)} %bitcast.67), kind=kLoop, calls=%fused_computation.99 | loop fusion | bytes 4194304 | tf_op jit(solution)/shard_map/slice | solution.py:15
  24.4 2.5 collective-permute-start
  30.6 59.0 %all-reduce.4.cloned.1.call-done = f32[8,16,256]{2,1,0:T(8,128)} async-done(((f32[8,16,256]{2,1,0:T(8,128)}), f32[8,16,256]{2,1,0:T(8,128)}) %all-reduce.4.cloned.1.call-update) | async-done | bytes 131088 | tf_op jit(solution)/shard_map/psum | solution.py:39
  94.6 34.3 %fusion.5 = f32[4,32,8,16,256]{4,3,2,1,0:T(8,128)} fusion(f32[4,32,8,16,256]{4,3,2,1,0:T(8,128)} %bitcast.68, f32[4,32,8,1,256]{4,3,2,1,0:T(1,128)S(1)} %copy.239, f32[4,32,8,1,256]{4,3,2,1,0:T(1,128)S(1)} %copy.237, f32[4]{0:T(128)S(1)} %get-tuple-element.31, f32[4]{0:T(128)S(1)} %get-tuple-element.33, f32[4]{0:T(128)S(1)} %get-tuple-element.30, ...), kind=kLoop, calls=%fused_computation.11 | loop fusion | flops 67108864 | bytes 39846080 | tf_op jit(solution)/shard_map/sub | solution.py:53
  128.9 9.2 %fusion.36 = (f32[2,32,8,16,256]{4,3,2,1,0:T(8,128)}, f32[2,32,8,16,256]{4,3,2,1,0:T(8,128)S(1)}) fusion(f32[4,32,8,16,256]{4,3,2,1,0:T(8,128)} %fusion.5), kind=kLoop, calls=%fused_computation.98 | loop fusion | bytes 33554432 | tf_op jit(solution)/shard_map/slice | solution.py:79
  140.1 3.0 fusion.38
  143.2 3.4 copy-done.2
  146.6 2.5 squeeze.36
  149.0 2.4 squeeze.37
  151.4 2.4 squeeze.38
  160.2 4.9 add_divide_fusion.7
  168.4 5.9 %copy.244 = f32[2,32,4096]{1,0,2:T(2,128)} copy(f32[2,32,4096]{2,1,0:T(8,128)} %add_divide_fusion.7) | data formatting | bytes 2097152 | tf_op jit(solution)/shard_map/div | solution.py:62
  174.3 5.7 %gather_fusion.1 = f32[1024,2,32]{2,1,0:T(2,128)S(1)} fusion(f32[2,32,4096]{1,0,2:T(2,128)} %copy.244, s32[1024]{0:T(1024)S(1)} %get-tuple-element.27), kind=kCustom, calls=%fused_computation.1 | custom fusion | bytes 528384 | tf_op jit(solution)/shard_map/gather | solution.py:74
  180.0 108.7 %all-gather.2.cloned.1.call-done = f32[16,32,4096]{2,1,0:T(8,128)} async-done(((f32[2,32,4096]{2,1,0:T(8,128)}), f32[16,32,4096]{2,1,0:T(8,128)}) %all-gather.2.cloned.1.call-update) | async-done | bytes 8388624 | tf_op jit(solution)/shard_map/all_gather | solution.py:68
  288.8 23.2 %copy.241 = f32[16,32,4096]{1,0,2:T(8,128)} copy(f32[16,32,4096]{2,1,0:T(8,128)} %all-gather.2.cloned.1.call-done) | data formatting | bytes 16777216 | tf_op jit(solution)/shard_map/all_gather | solution.py:68
  312.0 19.9 %gather_fusion = f32[1024,16,32]{2,1,0:T(8,128)} fusion(f32[16,32,4096]{1,0,2:T(8,128)} %copy.241, s32[1024]{0:T(1024)S(1)} %get-tuple-element.27), kind=kCustom, calls=%fused_computation | custom fusion | bytes 4198400 | tf_op jit(solution)/shard_map/gather | solution.py:69
  331.9 20.5 %gather_fusion.2 = f32[2048,32]{1,0:T(8,128)S(1)} fusion(f32[1024,16,32]{2,1,0:T(8,128)} %gather_fusion, s32[2048]{0:T(1024)S(1)} %reshape.137), kind=kCustom, calls=%fused_computation.2 | custom fusion | bytes 540672 | tf_op jit(solution)/shard_map/jit(take_along_axis)/gather | solution.py:71
  352.4 3.9 fusion.22
  356.4 93.7 %scatter_fusion = f32[2,32,4096]{1,0,2:T(2,128)} fusion(f32[2,32,4096]{1,0,2:T(2,128)} %copy.244, s32[1024]{0:T(1024)S(1)} %get-tuple-element.28, f32[1024,2,32]{2,1,0:T(2,128)S(1)} %fusion.22), kind=kCustom, calls=%fused_computation.3 | custom fusion | bytes 790528 | tf_op jit(solution)/shard_map/scatter | solution.py:75
  450.1 5.8 %broadcast_multiply_fusion = f32[2,32,4096]{1,0,2:T(2,128)} fusion(f32[2,32,4096]{1,0,2:T(2,128)} %scatter_fusion), kind=kLoop, calls=%fused_computation.22 | loop fusion | flops 262144 | bytes 2097152 | tf_op jit(solution)/shard_map/mul | solution.py:75
  455.9 3.6 copy.254
  470.1 6.9 %fusion.32 = (bf16[2,2,8,16,256]{4,3,2,1,0:T(8,128)(2,1)S(1)}, f32[2,2,32,8,16,256]{5,4,3,2,1,0:T(8,128)}) fusion(f32[2,1,32,8,16,256]{5,4,3,2,1,0:T(8,128)S(1)} %bitcast.76, f32[2,1,32,8,16,256]{5,4,3,2,1,0:T(8,128)S(1)} %bitcast.73), kind=kLoop, calls=%fused_computation.97 | loop fusion | flops 8257536 | bytes 33816576 | tf_op jit(solution)/shard_map/s,smzxy->zxy/reduce_sum | solution.py:88
  478.0 68.7 %all-reduce.6.cloned.1.call-done = f32[8,16,256]{2,1,0:T(8,128)} async-done(((f32[8,16,256]{2,1,0:T(8,128)}), f32[8,16,256]{2,1,0:T(8,128)}) %all-reduce.6.cloned.1.call-update) | async-done | bytes 131088 | tf_op jit(solution)/shard_map/psum | solution.py:88
  (86 shorter events, 33.9 us)
Async XLA Ops:
  7.2 22.2 %copy-start = (f32[3,32]{1,0:T(4,128)S(1)}, f32[3,32]{1,0:T(4,128)}, u32[]{:S(2)}) copy-start(f32[3,32]{1,0:T(4,128)} %param.11) | copy-start | bytes 1156
  7.2 82.4 %all-reduce.4.cloned.1.call-start = ((), (), s32[]{:S(2)}) async-start(), calls=%async_computation | async-start | bytes 262144 | tf_op jit(solution)/shard_map/psum | solution.py:39
  7.2 7.9 %copy-start.9 = (f32[32]{0:T(128)S(1)}, f32[32]{0:T(128)}, u32[]{:S(2)}) copy-start(f32[32]{0:T(128)} %param.15) | copy-start | bytes 388
  15.1 14.4 %copy-start.4 = (f32[16,256]{1,0:T(8,128)S(1)}, f32[16,256]{1,0:T(8,128)}, u32[]{:S(2)}) copy-start(f32[16,256]{1,0:T(8,128)} %param.16) | copy-start | bytes 49156
  15.1 14.4 %copy-start.7 = (f32[32]{0:T(128)S(1)}, f32[32]{0:T(128)}, u32[]{:S(2)}) copy-start(f32[32]{0:T(128)} %param.12) | copy-start | bytes 388
  15.1 14.4 %copy-start.5 = (f32[32]{0:T(128)S(1)}, f32[32]{0:T(128)}, u32[]{:S(2)}) copy-start(f32[32]{0:T(128)} %param.14) | copy-start | bytes 388
  15.1 15.3 %copy-start.8 = (f32[32]{0:T(128)S(1)}, f32[32]{0:T(128)}, u32[]{:S(2)}) copy-start(f32[32]{0:T(128)} %param.13) | copy-start | bytes 388
  16.2 272.6 %all-gather.2.cloned.1.call-start = ((), (), s32[]{:S(2)}) async-start(), calls=%async_computation.1 | async-start | bytes 9437184 | tf_op jit(solution)/shard_map/all_gather | solution.py:68
  24.4 66.8 %collective-permute-start = (f32[4,32,8,1,256]{4,2,3,1,0:T(8,128)S(1)}, f32[4,32,8,1,256]{4,2,3,1,0:T(8,128)S(1)}, u32[]{:S(2)}, u32[]{:S(2)}) collective-permute-start(f32[4,32,8,1,256]{4,2,3,1,0:T(8,128)S(1)} %copy.236), channel_id=1, source_target_pairs={{0,8},{8,16},{16,24},{1,9},{9,17},{17,25},{2,10},{10,18},{18,26},{... | collective-permute-start | bytes 3145736 | tf_op jit(solution)/shard_map/ppermute | solution.py:14
  27.9 64.4 %collective-permute-start.1 = (f32[4,32,8,1,256]{4,2,3,1,0:T(8,128)}, f32[4,32,8,1,256]{4,2,3,1,0:T(8,128)}, u32[]{:S(2)}, u32[]{:S(2)}) collective-permute-start(f32[4,32,8,1,256]{4,2,3,1,0:T(8,128)} %copy.238), channel_id=1, source_target_pairs={{8,0},{16,8},{24,16},{9,1},{17,9},{25,17},{10,2},{18,10},{26,18},{... | collective-permute-start | bytes 3145736 | tf_op jit(solution)/shard_map/ppermute | solution.py:17
  143.2 3.4 copy-start.2
  146.5 12.1 %copy-start.3 = (f32[2,32,1,16,256]{4,3,2,1,0:T(8,128)S(1)}, f32[2,32,1,16,256]{4,3,2,1,0:T(8,128)}, u32[]{:S(2)}) copy-start(f32[2,32,1,16,256]{4,3,2,1,0:T(8,128)} %get-tuple-element.21) | copy-start | bytes 3145732
  159.8 8.6 %copy-start.6 = (s32[1024]{0:T(1024)S(1)}, s32[1024]{0:T(1024)}, u32[]{:S(2)}) copy-start(s32[1024]{0:T(1024)} %param.17) | copy-start | bytes 12292
  165.0 381.6 %all-reduce.6.cloned.1.call-start = ((), (), s32[]{:S(2)}) async-start(), calls=%async_computation.2 | async-start | bytes 262144 | tf_op jit(solution)/shard_map/psum | solution.py:88
  459.4 7.1 %slice-start = ((s8[8388608]{0:T(1024)(128)(4,1)}), s8[4194304]{0:T(1024)(128)(4,1)S(1)}, s32[]{:S(2)}) async-start(s8[8388608]{0:T(1024)(128)(4,1)} %bitcast.69), calls=%async_computation.3 | async-start | bytes 8388608
  463.0 3.6 slice-start.1
  466.5 2.2 slice-start.2
  466.8 3.3 slice-start.3
  470.1 78.1 %copy-start.1 = (f32[3,32]{1,0:T(4,128)S(1)}, f32[3,32]{1,0:T(4,128)}, u32[]{:S(2)}) copy-start(f32[3,32]{1,0:T(4,128)} %param.11) | copy-start | bytes 1156
Sparse Core Ops, SparseCore 0:
  16.3 73.2 all-reduce.3
  165.2 123.5 all-gather.1
  478.1 68.4 all-reduce.5
where the time goes:
time: 558 us; the launch traced here: 555 us
  waiting for transfers between devices  236 us (42%)
  local copies, waits for them, and re-layouts  216 us (39%)
  other arithmetic  82.2 us (15%)
  between operations  14.8 us (3%)
    all_gather x1, waiting for transfers between devices, per_device(): everything = lax.all_gather(bottom, 'mode', axis=0, tiled=True)  109 us
    scatter x1, local copies, waits for them, and re-layouts, per_device(): bottom.at[:, :, rough_cells]  93.7 us
    psum x1, waiting for transfers between devices, per_device(): lax.psum(jnp.einsum('s,smzxy->zxy', weight_local, fresh), 'mode') / PAIRS  68.7 us
    psum x1, waiting for transfers between devices, per_device(): energy = lax.psum(partial_value, 'mode') / PAIRS  59 us
    sub x1, other arithmetic, per_device(): rhs = field + source[None] - speed * (along + across)  34.3 us
    all_gather x1, local copies, waits for them, and re-layouts, per_device(): everything = lax.all_gather(bottom, 'mode', axis=0, tiled=True)  23.2 us
    gather x3, local copies, waits for them, and re-layouts, per_device(): jnp.take_along_axis(values.transpose(2, 0, 1), targets[:, :, None], axis=1)  21 us
    gather x1, local copies, waits for them, and re-layouts, per_device(): values = everything[:, :, rough_cells]  19.9 us
  transfers between devices with their start and end apart: 5, of which 3 were waited for; matrix products, arithmetic and copies ran while one was open for 5% of the time, Pallas kernels for 0%

commit v1 on v0

v1 whole, which is shorter than its diff:
```python
import functools

import jax
import jax.numpy as jnp
from jax import lax
from jax.experimental import pallas as pl
from jax.experimental.pallas import tpu as pltpu
from jax.sharding import PartitionSpec as P

MESH = pl.DeviceIdType.MESH
F32 = jnp.float32
BF16 = jnp.bfloat16


def whole(space=pltpu.VMEM):
    return pl.BlockSpec(memory_space=space)


def squash(energy):
    return energy / (1.0 + 0.3 * jnp.abs(energy))


def send(src, dst, ssem, rsem, axis, target):
    return pltpu.make_async_remote_copy(
        src_ref=src,
        dst_ref=dst,
        send_sem=ssem,
        recv_sem=rsem,
        device_id={axis: target},
        device_id_type=MESH,
    )


def reduce_all(acc, slots, part, total, sems, n, finish):
    me = lax.axis_index("mode")
    rows = acc.shape[0] // n

    def chunk(i):
        return pl.ds(pl.multiple_of(i * rows, rows), rows)

    first = []
    for off in range(1, n):
        target = lax.rem(me + off, n)
        copy = send(
            acc.at[chunk(target)], slots.at[off], sems.at[0, off], sems.at[1, off], "mode", target
        )
        copy.start()
        first.append(copy)
    for copy in first:
        copy.wait_recv()
    value = acc[chunk(me), :]
    for off in range(1, n):
        value = value + slots[off]
    part[...] = finish(value)
    second = []
    for off in range(1, n):
        target = lax.rem(me + off, n)
        copy = send(part, total.at[chunk(me)], sems.at[2, off], sems.at[3, off], "mode", target)
        copy.start()
        second.append(copy)
    total[chunk(me), :] = part[...]
    for copy in first:
        copy.wait_send()
    for off in range(1, n):
        source = lax.rem(me + n - off, n)
        send(
            part, total.at[chunk(source)], sems.at[2, off], sems.at[3, off], "mode", source
        ).wait_recv()
    for copy in second:
        copy.wait_send()


def greet_modes(barrier, n):
    me = lax.axis_index("mode")
    for off in range(1, n):
        pl.semaphore_signal(
            barrier, inc=1, device_id={"mode": lax.rem(me + off, n)}, device_id_type=MESH
        )


def open_kernel(
    n, ns, modes, planes, pairs_total,
    weight, x_ref, equil, lo_out, hi_out,
    acc, slots, part, total, row_first, row_last, hsem, sems,
):
    step = pl.program_id(0)
    steps = pl.num_programs(0)
    block = x_ref.shape[0]
    rows = x_ref.shape[1]
    per_plane = rows // planes
    me = lax.axis_index("mode")
    sp = lax.axis_index("space")
    dirs_local = lo_out.shape[0] // modes

    @pl.when(step == 0)
    def _():
        barrier = pltpu.get_barrier_semaphore()
        greet_modes(barrier, n)

        @pl.when(sp > 0)
        def _():
            pl.semaphore_signal(barrier, inc=1, device_id={"space": sp - 1}, device_id_type=MESH)

        @pl.when(sp < ns - 1)
        def _():
            pl.semaphore_signal(barrier, inc=1, device_id={"space": sp + 1}, device_id_type=MESH)

        low = jnp.where(sp > 0, 1, 0)
        high = jnp.where(sp < ns - 1, 1, 0)
        pl.semaphore_wait(barrier, n - 1 + low + high)
        acc[...] = jnp.zeros_like(acc)

    part_of = pl.ds(step * block, block)
    has_low = jnp.where(sp > 0, 1.0, 0.0)
    has_high = jnp.where(sp < ns - 1, 1.0, 0.0)

    def edges(p, carry):
        for z in range(planes):
            first, last = z * per_plane, (z + 1) * per_plane - 1
            row_first[step * block + p, pl.ds(z, 1), :] = x_ref[p, pl.ds(first, 1), :] * has_low
            row_last[step * block + p, pl.ds(z, 1), :] = x_ref[p, pl.ds(last, 1), :] * has_high
        return carry

    lax.fori_loop(0, block, edges, 0)

    def down_copy(g):
        where = pl.ds(g * block, block)
        return send(
            row_first.at[where], hi_out.at[where], hsem.at[0, g], hsem.at[1, g], "space",
            lax.rem(sp + ns - 1, ns),
        )

    def up_copy(g):
        where = pl.ds(g * block, block)
        return send(
            row_last.at[where], lo_out.at[where], hsem.at[2, g], hsem.at[3, g], "space",
            lax.rem(sp + 1, ns),
        )

    def low_zero(g):
        where = pl.ds(g * block, block)
        return pltpu.make_async_copy(row_first.at[where], lo_out.at[where], hsem.at[3, g])

    def high_zero(g):
        where = pl.ds(g * block, block)
        return pltpu.make_async_copy(row_last.at[where], hi_out.at[where], hsem.at[1, g])

    @pl.when(sp > 0)
    def _():
        down_copy(step).start()

    @pl.when(sp == 0)
    def _():
        low_zero(step).start()

    @pl.when(sp < ns - 1)
    def _():
        up_copy(step).start()

    @pl.when(sp == ns - 1)
    def _():
        high_zero(step).start()

    w = weight[me * dirs_local + step * block // modes]

    def add_rows(r, carry):
        here = pl.ds(pl.multiple_of(r * 8, 8), 8)
        value = x_ref[0, here, :]
        for p in range(1, block):
            value = value + x_ref[p, here, :]
        acc[here, :] += w * value
        return carry

    lax.fori_loop(0, rows // 8, add_rows, 0)

    @pl.when(step == steps - 1)
    def _():
        reduce_all(
            acc, slots, part, total, sems, n, lambda value: squash(value * (1.0 / pairs_total))
        )
        equil[...] = total[...]

        def finish(g, carry):
            @pl.when(sp > 0)
            def _():
                down_copy(g).wait_send()
                up_copy(g).wait_recv()

            @pl.when(sp == 0)
            def _():
                low_zero(g).wait()

            @pl.when(sp < ns - 1)
            def _():
                up_copy(g).wait_send()
                down_copy(g).wait_recv()

            @pl.when(sp == ns - 1)
            def _():
                high_zero(g).wait()

            return carry

        lax.fori_loop(0, lo_out.shape[0] // block, finish, 0)


def open_step(x, weight, n, ns, modes, planes, pairs_total):
    pairs, rows, width = x.shape
    block = 16
    halo = jax.ShapeDtypeStruct((pairs, planes, width), F32)
    return pl.pallas_call(
        functools.partial(open_kernel, n, ns, modes, planes, pairs_total),
        grid=(pairs // block,),
        out_shape=(jax.ShapeDtypeStruct((rows, width), F32), halo, halo),
        in_specs=[whole(pltpu.SMEM), pl.BlockSpec((block, rows, width), lambda i: (i, 0, 0))],
        out_specs=(pl.BlockSpec((rows, width), lambda i: (0, 0)), whole(pl.ANY), whole(pl.ANY)),
        scratch_shapes=[
            pltpu.VMEM((rows, width), F32),
            pltpu.VMEM((n, rows // n, width), F32),
            pltpu.VMEM((rows // n, width), F32),
            pltpu.VMEM((rows, width), F32),
            pltpu.VMEM((pairs, planes, width), F32),
            pltpu.VMEM((pairs, planes, width), F32),
            pltpu.SemaphoreType.DMA((4, pairs // block)),
            pltpu.SemaphoreType.DMA((4, n)),
        ],
        compiler_params=pltpu.CompilerParams(collective_id=0, has_side_effects=True),
        name="open_step",
    )(weight, x)


def close_kernel(n, pairs_total, x_ref, out, slots, part, total, sems):
    barrier = pltpu.get_barrier_semaphore()
    greet_modes(barrier, n)
    pl.semaphore_wait(barrier, n - 1)
    reduce_all(x_ref, slots, part, total, sems, n, lambda value: value * (1.0 / pairs_total))
    out[...] = total[...]


def close_step(x, n, pairs_total):
    rows, width = x.shape
    return pl.pallas_call(
        functools.partial(close_kernel, n, pairs_total),
        out_shape=jax.ShapeDtypeStruct((rows, width), F32),
        in_specs=[whole()],
        out_specs=whole(),
        scratch_shapes=[
            pltpu.VMEM((n, rows // n, width), F32),
            pltpu.VMEM((rows // n, width), F32),
            pltpu.VMEM((rows, width), F32),
            pltpu.SemaphoreType.DMA((4, n)),
        ],
        compiler_params=pltpu.CompilerParams(collective_id=1, has_side_effects=True),
        name="close_step",
    )(x)


def split(value):
    high = value.astype(BF16)
    return high, (value - high.astype(F32)).astype(BF16)


def rough_kernel(n, count, bottom, cells, targets, inflow, held, picked, marks, ssem, rsem):
    me = lax.axis_index("mode")
    pairs, rows, width = bottom.shape
    slots = cells.shape[1]
    half = targets.shape[0]
    modes = pairs // half

    def place_of(index):
        return jnp.where(lax.rem(index, 2) == 0, index // 2, n - 1 - index // 2)

    def index_of(place):
        place = lax.rem(place + n, n)
        return jnp.where(place < n // 2, 2 * place, 2 * (n - 1 - place) + 1)

    place = place_of(me)
    ends = (index_of(place + 1), index_of(place - 1))
    barrier = pltpu.get_barrier_semaphore()
    for target in ends:
        pl.semaphore_signal(barrier, inc=1, device_id={"mode": target}, device_id_type=MESH)

    marks[...] = jnp.where(
        lax.broadcasted_iota(jnp.int32, (width, slots), 0) == lax.rem(cells[...], width), 1.0, 0.0
    ).astype(BF16)
    row_of = cells[...] // width
    on_row = jnp.where(lax.broadcasted_iota(jnp.int32, (rows, slots), 0) == row_of, 1.0, 0.0)

    group = min(16, pairs)

    def gather(g, carry):
        here = pl.ds(pl.multiple_of(g * group, group), group)
        high, low = split(bottom[here].reshape(group * rows, width))
        column = marks[...]
        got = jnp.dot(high, column, preferred_element_type=F32) + jnp.dot(
            low, column, preferred_element_type=F32
        )
        held[place, here, :] = jnp.sum(got.reshape(group, rows, slots) * on_row[None], axis=1)
        return carry

    lax.fori_loop(0, pairs // group, gather, 0)
    pl.semaphore_wait(barrier, 2)

    piece = pairs // 4

    def copy_of(way, part, step):
        slot = lax.rem(place + n + (-step if way == 0 else step), n)
        at = held.at[slot, pl.ds((2 * way + part) * piece, piece)]
        return send(at, at, ssem.at[way, part, step], rsem.at[way, part, step], "mode", ends[way])

    for step in range(n - 1):
        for part in range(2):
            for way in range(2):
                if step > 0:
                    arrived(copy_of, n, place, held, ssem, rsem, way, part, step - 1, piece, ends)
                copy_of(way, part, step).start()
    for part in range(2):
        for way in range(2):
            arrived(copy_of, n, place, held, ssem, rsem, way, part, n - 2, piece, ends)
    for step in range(n - 1):
        for part in range(2):
            for way in range(2):
                copy_of(way, part, step).wait_send()

    for h in range(half):
        want = targets[pl.ds(h, 1), :]
        for m in range(0, modes, 8):
            value = jnp.zeros((8, slots), F32)
            for p in range(n):
                owner = 2 * p if p < n // 2 else 2 * (n - 1 - p) + 1
                for j in range(half):
                    value = jnp.where(
                        want == owner * half + j, held[p, pl.ds(j * modes + m, 8), :], value
                    )
            picked[pl.ds(h * modes + m, 8), :] = value

    live = jnp.where(lax.broadcasted_iota(jnp.int32, (rows, slots), 1) < count[0], on_row, 0.0)
    contract = (((1,), (1,)), ((), ()))
    is_rough = lax.dot_general(live.astype(BF16), marks[...], contract, preferred_element_type=F32)
    is_rough = (is_rough > 0.5)[None]

    def scatter(g, carry):
        here = pl.ds(pl.multiple_of(g * group, group), group)
        spread = (picked[here, :][:, None, :] * live[None]).reshape(group * rows, slots)
        high, low = split(spread)
        column = marks[...]
        put = lax.dot_general(
            high, column, contract, preferred_element_type=F32
        ) + lax.dot_general(low, column, contract, preferred_element_type=F32)
        inflow[here] = 0.9 * jnp.where(is_rough, put.reshape(group, rows, width), bottom[here])
        return carry

    lax.fori_loop(0, pairs // group, scatter, 0)


def arrived(copy_of, n, place, held, ssem, rsem, way, part, step, piece, ends):
    slot = lax.rem(place + n + (-step - 1 if way == 0 else step + 1), n)
    at = held.at[slot, pl.ds((2 * way + part) * piece, piece)]
    send(
        at, at, ssem.at[way, part, step], rsem.at[way, part, step], "mode", ends[way]
    ).wait_recv()


def rough_step(bottom, cells, count, targets, n):
    pairs, rows, width = bottom.shape
    slots = cells.shape[1]
    return pl.pallas_call(
        functools.partial(rough_kernel, n),
        out_shape=jax.ShapeDtypeStruct(bottom.shape, F32),
        in_specs=[whole(pltpu.SMEM), whole(), whole(), whole()],
        out_specs=whole(),
        scratch_shapes=[
            pltpu.VMEM((n, pairs, slots), F32),
            pltpu.VMEM((pairs, slots), F32),
            pltpu.VMEM((width, slots), BF16),
            pltpu.SemaphoreType.DMA((2, 2, n - 1)),
            pltpu.SemaphoreType.DMA((2, 2, n - 1)),
        ],
        compiler_params=pltpu.CompilerParams(collective_id=2, has_side_effects=True),
        name="rough_step",
    )(count, bottom, cells, targets)


def sweep_kernel(down, planes, *refs):
    if down:
        (dir_cos, velocity, rate, spectrum, weight, x_ref, lo, hi, equil, start, out, bottom,
         energy) = refs
    else:
        (dir_cos, velocity, rate, spectrum, weight, x_ref, lo, hi, equil, start, before, _,
         out, energy) = refs
    h, b = pl.program_id(0), pl.program_id(1)
    count, total_rows, width = x_ref.shape
    rows = total_rows // planes

    @pl.when((h == 0) & (b == 0))
    def _():
        energy[...] = jnp.zeros_like(energy) if down else before[...]

    s = (lax.axis_index("mode") * pl.num_programs(0) + h) * 2 + (1 if down else 0)
    cx, cy, cz = dir_cos[0, s], dir_cos[1, s], dir_cos[2, s]
    w = weight[s]
    row = lax.broadcasted_iota(jnp.int32, (rows, width), 0)
    lane = lax.broadcasted_iota(jnp.int32, (rows, width), 1)

    def run(low_x, low_y):
        def one(i, carry):
            m = b * count + i
            v = velocity[m]
            c = v * jnp.abs(cz)
            inv = 1.0 / jnp.full((rows, width), 1.0 + rate[m] + c, F32)
            vx, vy = v * jnp.abs(cx), v * jnp.abs(cy)
            k_own, k_x, k_y = inv * (1.0 - vx - vy), inv * vx, inv * vy
            k_src, k_prev = inv * (rate[m] * spectrum[m]), inv * c
            k_y = jnp.where(lane == (0 if low_y else width - 1), 0.0, k_y)
            if down:
                value = start[...] * spectrum[m]
            else:
                value = start[i]
            for z in reversed(range(planes)) if down else range(planes):
                here = pl.ds(z * rows, rows)
                own = x_ref[i, here, :]
                edge = (lo if low_x else hi)[i, pl.ds(z, 1), :]
                if low_x:
                    side = jnp.where(row == 0, edge, pltpu.roll(own, 1, 0))
                else:
                    side = jnp.where(row == rows - 1, edge, pltpu.roll(own, rows - 1, 0))
                along = pltpu.roll(own, 1 if low_y else width - 1, 1)
                value = (
                    k_own * own + k_x * side + k_y * along + k_src * equil[here, :]
                    + k_prev * value
                )
                out[i, here, :] = value
                energy[here, :] += w * value
            if down:
                bottom[i] = value
            return carry

        lax.fori_loop(0, count, one, 0)

    for low_x in (True, False):
        for low_y in (True, False):
            @pl.when(((cx >= 0) == low_x) & ((cy >= 0) == low_y))
            def _():
                run(low_x, low_y)


def sweep_step(down, planes, scalars, x, lo, hi, equil, start, before=None, aliased=None):
    half, _, modes, total_rows, width = x.shape
    rows = total_rows // planes
    block = min(8, modes)
    side = 1 if down else 0
    big = pl.BlockSpec((None, None, block, total_rows, width), lambda h, b: (h, side, b, 0, 0))
    edge = pl.BlockSpec((None, None, block, planes, width), lambda h, b: (h, side, b, 0, 0))
    flat = pl.BlockSpec((total_rows, width), lambda h, b: (0, 0))
    floor = pl.BlockSpec((None, block, rows, width), lambda h, b: (h, b, 0, 0))
    heat = pl.BlockSpec((rows, width), lambda h, b: (0, 0))
    in_specs = [whole(pltpu.SMEM)] * len(scalars) + [big, edge, edge, flat]
    flat_shape = jax.ShapeDtypeStruct((total_rows, width), F32)
    floor_shape = jax.ShapeDtypeStruct((half, modes, rows, width), F32)
    args = [*scalars, x, lo, hi, equil, start]
    if down:
        in_specs += [heat]
        out_shape = (jax.ShapeDtypeStruct(x.shape, F32), floor_shape, flat_shape)
        out_specs = (big, floor, flat)
        aliases = {}
    else:
        in_specs += [floor, flat, whole(pl.ANY)]
        args += [before, aliased]
        out_shape = (jax.ShapeDtypeStruct(x.shape, F32), flat_shape)
        out_specs = (big, flat)
        aliases = {len(args) - 1: 0}
    return pl.pallas_call(
        functools.partial(sweep_kernel, down, planes),
        grid=(half, modes // block),
        out_shape=out_shape,
        in_specs=in_specs,
        out_specs=out_specs,
        input_output_aliases=aliases,
        name="down_sweep" if down else "up_sweep",
    )(*args)


def per_device(
    n, ns, intensity, dir_cos, velocity, rate, spectrum, weight, heat, rough_cells, rough_count,
    rough_map,
):
    pairs, planes, rows, width = intensity.shape
    modes = velocity.shape[0]
    half = pairs // modes // 2
    pairs_total = pairs * n
    position = lax.axis_index("mode")
    flat = intensity.reshape(pairs, planes * rows, width)
    equil, lo, hi = open_step(flat, weight, n, ns, modes, planes, pairs_total)
    x = intensity.reshape(half, 2, modes, planes * rows, width)
    lo = lo.reshape(half, 2, modes, planes, width)
    hi = hi.reshape(half, 2, modes, planes, width)
    scalars = (dir_cos, velocity, rate, spectrum, weight)
    fresh, bottom, energy = sweep_step(True, planes, scalars, x, lo, hi, equil, heat)
    targets = lax.dynamic_slice_in_dim(rough_map, position * half, half, 1).T
    inflow = rough_step(
        bottom.reshape(half * modes, rows, width), rough_cells[None], rough_count, targets, n
    )
    inflow = inflow.reshape(half, modes, rows, width)
    fresh, energy = sweep_step(
        False, planes, scalars, x, lo, hi, equil, inflow, energy, fresh
    )
    energy = close_step(energy, n, pairs_total)
    return fresh.reshape(intensity.shape), energy.reshape(planes, rows, width)


def solution(mesh):
    n, ns = mesh.shape["mode"], mesh.shape["space"]
    in_specs = (
        P("mode", None, "space", None),
        P(),
        P(),
        P(),
        P(),
        P(),
        P("space", None),
        P("space"),
        P("space"),
        P("space", None),
    )
    out_specs = (P("mode", None, "space", None), P(None, "space", None))
    return jax.shard_map(
        functools.partial(per_device, n, ns),
        mesh=mesh,
        in_specs=in_specs,
        out_specs=out_specs,
        check_vma=False,
    )
```

time: 558 us -> 104 us (0.19)
  waiting for transfers between devices: 236 us -> 0 us
  local copies, waits for them, and re-layouts: 216 us -> 2.32 us
  Pallas kernels: 0 us -> 99.2 us
  other arithmetic: 82.2 us -> 0 us
  between operations: 14.8 us -> 1.35 us
    psum x2 -> x0, waiting for transfers between devices: 128 us -> none  [the longest x1 68.7 us: per_device(): lax.psum(jnp.einsum('s,smzxy->zxy', weight_local, fresh), 'mode') / PAIRS]
    all_gather x1 -> x0, waiting for transfers between devices: 109 us -> none  [per_device(): everything = lax.all_gather(bottom, 'mode', axis=0, tiled=True)]
    pallas_call x0 -> x5, Pallas kernels: none -> 99.2 us  [the longest x1 33.9 us: rough_step(): pl.pallas_call(functools.partial(rough_kernel, n), out_shape=jax.ShapeDty...]
    scatter x1 -> x0, local copies, waits for them, and re-layouts: 93.7 us -> none  [per_device(): bottom.at[:, :, rough_cells]]
    gather x5 -> x0, local copies, waits for them, and re-layouts: 46.7 us -> none  [the longest x3 21 us: per_device(): jnp.take_along_axis(values.transpose(2, 0, 1), targets[:, :, None], axis=1)]
    sub x1 -> x0, other arithmetic: 34.3 us -> none  [per_device(): rhs = field + source[None] - speed * (along + across)]
    all_gather x1 -> x0, local copies, waits for them, and re-layouts: 23.2 us -> none  [per_device(): everything = lax.all_gather(bottom, 'mode', axis=0, tiled=True)]
    slice x6 -> x0, local copies, waits for them, and re-layouts: 18.4 us -> none  [the longest x1 9.22 us: per_device(): up_rhs = rhs[0::2]]
  transfers between devices with their start and end apart: 5 -> 0, of which waited for: 3 -> 0; matrix products, arithmetic and copies ran while one was open for 5% -> 0% of each run, Pallas kernels for 0% -> 0%
where the time goes in v1:
time: 104 us; the launch traced here: 103 us
  Pallas kernels  99.2 us (95%)
  local copies, waits for them, and re-layouts  2.32 us (2%)
  between operations  1.35 us (1%)
    pallas_call x1, Pallas kernels, rough_step(): pl.pallas_call(functools.partial(rough_kernel, n), out_shape=jax.ShapeDty...  33.9 us
    pallas_call x1, Pallas kernels, open_step(): pl.pallas_call(functools.partial(open_kernel, n, ns, modes, planes, pairs...  26.6 us
    pallas_call x2, Pallas kernels, sweep_step(): pl.pallas_call(functools.partial(sweep_kernel, down, planes), grid=(half,...  25.3 us
    pallas_call x1, Pallas kernels, close_step(): pl.pallas_call(functools.partial(close_kernel, n, pairs_total), out_shape...  13.4 us

profile of v1, /device:TPU:0, one launch (start us, length us, event | category | flops | bytes accessed | tf_op | source)
XLA Modules:
  0.0 102.8 jit_solution(2482208848487778337)
XLA Ops:
  0.6 0.0 copy-start
  1.3 0.1 copy-done
  1.5 0.6 dynamic-slice_bitcast_fusion.targets
  2.1 26.6 %open_step.1 = (f32[128,256]{1,0:T(8,128)}, f32[128,8,256]{2,1,0:T(8,128)}, f32[128,8,256]{2,1,0:T(8,128)}) custom-call(f32[32]{0:T(128)} %refs_4_.3, f32[128,128,256]{2,1,0:T(8,128)} %bitcast.11), custom_call_target="tpu_custom_call" | custom-call | tf_op jit(solution)/shard_map/open_step/pallas_call | solution.py:211
  28.7 12.7 %down_sweep.1 = (f32[2,2,32,128,256]{4,3,2,1,0:T(8,128)}, f32[2,32,16,256]{3,2,1,0:T(8,128)}, f32[128,256]{1,0:T(8,128)}) custom-call(f32[3,32]{1,0:T(4,128)} %refs_0_.3, f32[32]{0:T(128)} %refs_1_.3, f32[32]{0:T(128)} %refs_2_.3, f32[32]{0:T(128)} %refs_3_.3, f32[32]{0:T(128)} %refs_4_.3, f32[2,2,32,128,256]{4,3,2,1,0:T(8,128)} %bitcast.12, ...), custom_call_target="tpu_custom_call" | custom-call | tf_op jit(solution)/shard_map/down_sweep/pallas_call | solution.py:472
  41.4 33.9 %rough_step.1 = f32[64,16,256]{2,1,0:T(8,128)} custom-call(s32[1]{0:T(128)S(6)} %copy.15.count, f32[64,16,256]{2,1,0:T(8,128)} %bitcast.20, s32[1,1024]{1,0:T(1,128)} %bitcast.22, s32[2,1024]{1,0:T(2,128)} %dynamic-slice_bitcast_fusion.targets), custom_call_target="tpu_custom_call" | custom-call | tf_op jit(solution)/shard_map/rough_step/pallas_call | solution.py:367
  75.3 12.6 %up_sweep.1 = (f32[2,2,32,128,256]{4,3,2,1,0:T(8,128)}, f32[128,256]{1,0:T(8,128)}) custom-call(f32[3,32]{1,0:T(4,128)} %refs_0_.3, f32[32]{0:T(128)} %refs_1_.3, f32[32]{0:T(128)} %refs_2_.3, f32[32]{0:T(128)} %refs_3_.3, f32[32]{0:T(128)} %refs_4_.3, f32[2,2,32,128,256]{4,3,2,1,0:T(8,128)} %bitcast.13, ...), custom_call_target="tpu_custom_call", output_to_operand_aliasing={{0}: (11, {})} | custom-call | tf_op jit(solution)/shard_map/up_sweep/pallas_call | solution.py:472
  87.9 13.4 %close_step.1 = f32[128,256]{1,0:T(8,128)} custom-call(f32[128,256]{1,0:T(8,128)} %get-tuple-element.17.x_ref), custom_call_target="tpu_custom_call" | custom-call | tf_op jit(solution)/shard_map/close_step/pallas_call | solution.py:242
  101.3 1.6 %copy.16 = f32[8,16,256]{2,1,0:T(8,128)} copy(f32[8,16,256]{2,1,0:T(8,128)} %bitcast.21) | data formatting | bytes 262144
Async XLA Ops:
  0.6 0.8 copy-start

commit v2 on v1

--- a/solution.py
+++ b/solution.py
@@ -286,54 +286,66 @@
     row_of = cells[...] // width
     on_row = jnp.where(lax.broadcasted_iota(jnp.int32, (rows, slots), 0) == row_of, 1.0, 0.0)
 
-    group = min(16, pairs)
-
-    def gather(g, carry):
-        here = pl.ds(pl.multiple_of(g * group, group), group)
-        high, low = split(bottom[here].reshape(group * rows, width))
+    piece = pairs // 4
+
+    def rows_of(way, part):
+        return (2 * way + part) * piece
+
+    def gather(first):
+        here = pl.ds(first, piece)
+        high, low = split(bottom[here].reshape(piece * rows, width))
         column = marks[...]
         got = jnp.dot(high, column, preferred_element_type=F32) + jnp.dot(
             low, column, preferred_element_type=F32
         )
-        held[place, here, :] = jnp.sum(got.reshape(group, rows, slots) * on_row[None], axis=1)
-        return carry
-
-    lax.fori_loop(0, pairs // group, gather, 0)
-    pl.semaphore_wait(barrier, 2)
-
-    piece = pairs // 4
+        held[place, here, :] = jnp.sum(got.reshape(piece, rows, slots) * on_row[None], axis=1)
+
+    def slot_of(way, step):
+        return lax.rem(place + n + (-step if way == 0 else step), n)
 
     def copy_of(way, part, step):
-        slot = lax.rem(place + n + (-step if way == 0 else step), n)
-        at = held.at[slot, pl.ds((2 * way + part) * piece, piece)]
+        at = held.at[slot_of(way, step), pl.ds(rows_of(way, part), piece)]
         return send(at, at, ssem.at[way, part, step], rsem.at[way, part, step], "mode", ends[way])
 
-    for step in range(n - 1):
+    def arrival(way, part, step):
+        at = held.at[slot_of(way, step + 1), pl.ds(rows_of(way, part), piece)]
+        return send(at, at, ssem.at[way, part, step], rsem.at[way, part, step], "mode", ends[way])
+
+    def choose(way, step):
+        slot = slot_of(way, step)
+        owner = index_of(slot)
+        for h in range(half):
+            want = targets[pl.ds(h, 1), :]
+            for first in range(rows_of(way, 0), rows_of(way, 0) + 2 * piece, 8):
+                j, m = first // modes, first % modes
+                here = pl.ds(h * modes + m, 8)
+                picked[here, :] = jnp.where(
+                    want == owner * half + j, held[slot, pl.ds(first, 8), :], picked[here, :]
+                )
+
+    for part in range(2):
+        for way in range(2):
+            gather(rows_of(way, part))
+            if part == 0 and way == 0:
+                pl.semaphore_wait(barrier, 2)
+            copy_of(way, part, 0).start()
+    picked[...] = jnp.zeros_like(picked)
+    for way in range(2):
+        choose(way, 0)
+    for step in range(1, n):
         for part in range(2):
             for way in range(2):
-                if step > 0:
-                    arrived(copy_of, n, place, held, ssem, rsem, way, part, step - 1, piece, ends)
-                copy_of(way, part, step).start()
-    for part in range(2):
+                arrival(way, part, step - 1).wait_recv()
+                if step < n - 1:
+                    copy_of(way, part, step).start()
         for way in range(2):
-            arrived(copy_of, n, place, held, ssem, rsem, way, part, n - 2, piece, ends)
+            choose(way, step)
     for step in range(n - 1):
         for part in range(2):
             for way in range(2):
                 copy_of(way, part, step).wait_send()
 
-    for h in range(half):
-        want = targets[pl.ds(h, 1), :]
-        for m in range(0, modes, 8):
-            value = jnp.zeros((8, slots), F32)
-            for p in range(n):
-                owner = 2 * p if p < n // 2 else 2 * (n - 1 - p) + 1
-                for j in range(half):
-                    value = jnp.where(
-                        want == owner * half + j, held[p, pl.ds(j * modes + m, 8), :], value
-                    )
-            picked[pl.ds(h * modes + m, 8), :] = value
-
+    group = piece
     live = jnp.where(lax.broadcasted_iota(jnp.int32, (rows, slots), 1) < count[0], on_row, 0.0)
     contract = (((1,), (1,)), ((), ()))
     is_rough = lax.dot_general(live.astype(BF16), marks[...], contract, preferred_element_type=F32)
@@ -351,14 +363,6 @@
         return carry
 
     lax.fori_loop(0, pairs // group, scatter, 0)
-
-
-def arrived(copy_of, n, place, held, ssem, rsem, way, part, step, piece, ends):
-    slot = lax.rem(place + n + (-step - 1 if way == 0 else step + 1), n)
-    at = held.at[slot, pl.ds((2 * way + part) * piece, piece)]
-    send(
-        at, at, ssem.at[way, part, step], rsem.at[way, part, step], "mode", ends[way]
-    ).wait_recv()
 
 
 def rough_step(bottom, cells, count, targets, n):
@@ -402,40 +406,51 @@
     row = lax.broadcasted_iota(jnp.int32, (rows, width), 0)
     lane = lax.broadcasted_iota(jnp.int32, (rows, width), 1)
 
+    wide = min(4, count)
+
     def run(low_x, low_y):
-        def one(i, carry):
-            m = b * count + i
-            v = velocity[m]
-            c = v * jnp.abs(cz)
-            inv = 1.0 / jnp.full((rows, width), 1.0 + rate[m] + c, F32)
-            vx, vy = v * jnp.abs(cx), v * jnp.abs(cy)
-            k_own, k_x, k_y = inv * (1.0 - vx - vy), inv * vx, inv * vy
-            k_src, k_prev = inv * (rate[m] * spectrum[m]), inv * c
-            k_y = jnp.where(lane == (0 if low_y else width - 1), 0.0, k_y)
-            if down:
-                value = start[...] * spectrum[m]
-            else:
-                value = start[i]
+        def some(g, carry):
+            picks = [g * wide + t for t in range(wide)]
+            own_k, x_k, y_k, src_k, prev_k, values = [], [], [], [], [], []
+            for i in picks:
+                m = b * count + i
+                v = velocity[m]
+                c = v * jnp.abs(cz)
+                inv = 1.0 / jnp.full((rows, width), 1.0 + rate[m] + c, F32)
+                vx, vy = v * jnp.abs(cx), v * jnp.abs(cy)
+                own_k.append(inv * (1.0 - vx - vy))
+                x_k.append(inv * vx)
+                y_k.append(inv * vy)
+                src_k.append(inv * (rate[m] * spectrum[m]))
+                prev_k.append(inv * c)
+                values.append(start[...] * spectrum[m] if down else start[i])
             for z in reversed(range(planes)) if down else range(planes):
                 here = pl.ds(z * rows, rows)
-                own = x_ref[i, here, :]
-                edge = (lo if low_x else hi)[i, pl.ds(z, 1), :]
-                if low_x:
-                    side = jnp.where(row == 0, edge, pltpu.roll(own, 1, 0))
-                else:
-                    side = jnp.where(row == rows - 1, edge, pltpu.roll(own, rows - 1, 0))
-                along = pltpu.roll(own, 1 if low_y else width - 1, 1)
-                value = (
-                    k_own * own + k_x * side + k_y * along + k_src * equil[here, :]
-                    + k_prev * value
-                )
-                out[i, here, :] = value
-                energy[here, :] += w * value
+                level = equil[here, :]
+                total = None
+                for t, i in enumerate(picks):
+                    own = x_ref[i, here, :]
+                    edge = (lo if low_x else hi)[i, pl.ds(z, 1), :]
+                    if low_x:
+                        side = jnp.where(row == 0, edge, pltpu.roll(own, 1, 0))
+                    else:
+                        side = jnp.where(row == rows - 1, edge, pltpu.roll(own, rows - 1, 0))
+                    along = pltpu.roll(own, 1 if low_y else width - 1, 1)
+                    along = jnp.where(lane == (0 if low_y else width - 1), 0.0, along)
+                    value = (
+                        own_k[t] * own + x_k[t] * side + y_k[t] * along + src_k[t] * level
+                        + prev_k[t] * values[t]
+                    )
+                    values[t] = value
+                    out[i, here, :] = value
+                    total = value if total is None else total + value
+                energy[here, :] += w * total
             if down:
-                bottom[i] = value
+                for t, i in enumerate(picks):
+                    bottom[i] = values[t]
             return carry
 
-        lax.fori_loop(0, count, one, 0)
+        lax.fori_loop(0, count // wide, some, 0)
 
     for low_x in (True, False):
         for low_y in (True, False):

time: 104 us -> 100 us (0.962)
  Pallas kernels: 99.2 us -> 95.9 us
    pallas_call x2, Pallas kernels: 25.3 us -> 23.2 us  [sweep_step(): pl.pallas_call(functools.partial(sweep_kernel, down, planes), grid=(half,...]
where the time goes in v2:
time: 100 us; the launch traced here: 99.6 us
  Pallas kernels  95.9 us (96%)
  local copies, waits for them, and re-layouts  2.32 us (2%)
  between operations  1.35 us (1%)
    pallas_call x1, Pallas kernels, rough_step(): pl.pallas_call(functools.partial(rough_kernel, n), out_shape=jax.ShapeDty...  33.1 us
    pallas_call x1, Pallas kernels, open_step(): pl.pallas_call(functools.partial(open_kernel, n, ns, modes, planes, pairs...  26.6 us
    pallas_call x2, Pallas kernels, sweep_step(): pl.pallas_call(functools.partial(sweep_kernel, down, planes), grid=(half,...  23.2 us
    pallas_call x1, Pallas kernels, close_step(): pl.pallas_call(functools.partial(close_kernel, n, pairs_total), out_shape...  13 us

profile of v2, /device:TPU:0, one launch (start us, length us, event | category | flops | bytes accessed | tf_op | source)
XLA Modules:
  0.0 99.6 jit_solution(13728825280781451070)
XLA Ops:
  0.6 0.0 copy-start
  1.3 0.1 copy-done
  1.5 0.6 dynamic-slice_bitcast_fusion.targets
  2.1 26.6 %open_step.1 = (f32[128,256]{1,0:T(8,128)}, f32[128,8,256]{2,1,0:T(8,128)}, f32[128,8,256]{2,1,0:T(8,128)}) custom-call(f32[32]{0:T(128)} %refs_4_.3, f32[128,128,256]{2,1,0:T(8,128)} %bitcast.11), custom_call_target="tpu_custom_call" | custom-call | tf_op jit(solution)/shard_map/open_step/pallas_call | solution.py:211
  28.7 11.7 %down_sweep.1 = (f32[2,2,32,128,256]{4,3,2,1,0:T(8,128)}, f32[2,32,16,256]{3,2,1,0:T(8,128)}, f32[128,256]{1,0:T(8,128)}) custom-call(f32[3,32]{1,0:T(4,128)} %refs_0_.3, f32[32]{0:T(128)} %refs_1_.3, f32[32]{0:T(128)} %refs_2_.3, f32[32]{0:T(128)} %refs_3_.3, f32[32]{0:T(128)} %refs_4_.3, f32[2,2,32,128,256]{4,3,2,1,0:T(8,128)} %bitcast.12, ...), custom_call_target="tpu_custom_call" | custom-call | tf_op jit(solution)/shard_map/down_sweep/pallas_call | solution.py:487
  40.4 33.1 %rough_step.1 = f32[64,16,256]{2,1,0:T(8,128)} custom-call(s32[1]{0:T(128)S(6)} %copy.15.count, f32[64,16,256]{2,1,0:T(8,128)} %bitcast.20, s32[1,1024]{1,0:T(1,128)} %bitcast.22, s32[2,1024]{1,0:T(2,128)} %dynamic-slice_bitcast_fusion.targets), custom_call_target="tpu_custom_call" | custom-call | tf_op jit(solution)/shard_map/rough_step/pallas_call | solution.py:371
  73.5 11.5 %up_sweep.1 = (f32[2,2,32,128,256]{4,3,2,1,0:T(8,128)}, f32[128,256]{1,0:T(8,128)}) custom-call(f32[3,32]{1,0:T(4,128)} %refs_0_.3, f32[32]{0:T(128)} %refs_1_.3, f32[32]{0:T(128)} %refs_2_.3, f32[32]{0:T(128)} %refs_3_.3, f32[32]{0:T(128)} %refs_4_.3, f32[2,2,32,128,256]{4,3,2,1,0:T(8,128)} %bitcast.13, ...), custom_call_target="tpu_custom_call", output_to_operand_aliasing={{0}: (11, {})} | custom-call | tf_op jit(solution)/shard_map/up_sweep/pallas_call | solution.py:487
  85.0 13.0 %close_step.1 = f32[128,256]{1,0:T(8,128)} custom-call(f32[128,256]{1,0:T(8,128)} %get-tuple-element.17.x_ref), custom_call_target="tpu_custom_call" | custom-call | tf_op jit(solution)/shard_map/close_step/pallas_call | solution.py:242
  98.0 1.6 %copy.16 = f32[8,16,256]{2,1,0:T(8,128)} copy(f32[8,16,256]{2,1,0:T(8,128)} %bitcast.21) | data formatting | bytes 262144
Async XLA Ops:
  0.6 0.8 copy-start

commit v3 on v2

--- a/solution.py
+++ b/solution.py
@@ -260,7 +260,10 @@
     return high, (value - high.astype(F32)).astype(BF16)
 
 
-def rough_kernel(n, count, bottom, cells, targets, inflow, held, picked, marks, ssem, rsem):
+def rough_kernel(
+    n, planes, count, dir_cos, velocity, rate, spectrum, bottom, cells, targets, equil, x, lo, hi,
+    inflow, base, held, picked, marks, xin, loin, hiin, xout, ssem, rsem, lsem,
+):
     me = lax.axis_index("mode")
     pairs, rows, width = bottom.shape
     slots = cells.shape[1]
@@ -323,6 +326,82 @@
                     want == owner * half + j, held[slot, pl.ds(first, 8), :], picked[here, :]
                 )
 
+    batch = xin.shape[1]
+    per_dir = modes // batch
+    chunks = half * per_dir
+    wide = min(4, batch)
+    row = lax.broadcasted_iota(jnp.int32, (rows, width), 0)
+    lane = lax.broadcasted_iota(jnp.int32, (rows, width), 1)
+
+    def loads(c):
+        at = (c // per_dir, 0, pl.ds((c % per_dir) * batch, batch))
+        return [
+            pltpu.make_async_copy(src.at[at], dst.at[c % 2], lsem.at[k, c % 2])
+            for k, (src, dst) in enumerate(((x, xin), (lo, loin), (hi, hiin)))
+        ]
+
+    def store(c):
+        at = (c // per_dir, pl.ds((c % per_dir) * batch, batch))
+        return pltpu.make_async_copy(xout.at[c % 2], base.at[at], lsem.at[3, c % 2])
+
+    def advance(c):
+        for copy in loads(c):
+            copy.wait()
+        if c + 1 < chunks:
+            for copy in loads(c + 1):
+                copy.start()
+        if c >= 2:
+            store(c - 2).wait()
+        slot = c % 2
+        s = (me * half + c // per_dir) * 2
+        cx, cy, cz = dir_cos[0, s], dir_cos[1, s], dir_cos[2, s]
+        low_x = jnp.full((rows, width), cx, F32) >= 0.0
+        low_y = jnp.full((rows, width), cy, F32) >= 0.0
+        at_edge = (low_x & (row == 0)) | (~low_x & (row == rows - 1))
+        at_side = (low_y & (lane == 0)) | (~low_y & (lane == width - 1))
+
+        def some(g, carry):
+            picks = [g * wide + t for t in range(wide)]
+            own_k, x_k, y_k, src_k, prev_k, values = [], [], [], [], [], [None] * wide
+            for i in picks:
+                m = (c % per_dir) * batch + i
+                v = velocity[m]
+                turn = v * jnp.abs(cz)
+                inv = 1.0 / jnp.full((rows, width), 1.0 + rate[m] + turn, F32)
+                vx, vy = v * jnp.abs(cx), v * jnp.abs(cy)
+                own_k.append(inv * (1.0 - vx - vy))
+                x_k.append(inv * vx)
+                y_k.append(inv * vy)
+                src_k.append(inv * (rate[m] * spectrum[m]))
+                prev_k.append(inv * turn)
+            for z in range(planes):
+                here = pl.ds(z * rows, rows)
+                level = equil[here, :]
+                for t, i in enumerate(picks):
+                    own = xin[slot, i, here, :]
+                    edge = jnp.where(
+                        low_x,
+                        jnp.broadcast_to(loin[slot, i, pl.ds(z, 1), :], (rows, width)),
+                        jnp.broadcast_to(hiin[slot, i, pl.ds(z, 1), :], (rows, width)),
+                    )
+                    side = jnp.where(low_x, pltpu.roll(own, 1, 0), pltpu.roll(own, rows - 1, 0))
+                    side = jnp.where(at_edge, edge, side)
+                    along = jnp.where(low_y, pltpu.roll(own, 1, 1), pltpu.roll(own, width - 1, 1))
+                    along = jnp.where(at_side, 0.0, along)
+                    value = (
+                        own_k[t] * own + x_k[t] * side + y_k[t] * along + src_k[t] * level
+                    )
+                    if values[t] is not None:
+                        value = value + prev_k[t] * values[t]
+                    values[t] = value
+                    xout[slot, i, here, :] = value
+            return carry
+
+        lax.fori_loop(0, batch // wide, some, 0)
+        store(c).start()
+
+    for copy in loads(0):
+        copy.start()
     for part in range(2):
         for way in range(2):
             gather(rows_of(way, part))
@@ -332,6 +411,8 @@
     picked[...] = jnp.zeros_like(picked)
     for way in range(2):
         choose(way, 0)
+    for c in range(0, chunks // n):
+        advance(c)
     for step in range(1, n):
         for part in range(2):
             for way in range(2):
@@ -340,11 +421,15 @@
                     copy_of(way, part, step).start()
         for way in range(2):
             choose(way, step)
+        for c in range(step * chunks // n, (step + 1) * chunks // n):
+            advance(c)
     for step in range(n - 1):
         for part in range(2):
             for way in range(2):
                 copy_of(way, part, step).wait_send()
 
+    for c in range(max(0, chunks - 2), chunks):
+        store(c).wait()
     group = piece
     live = jnp.where(lax.broadcasted_iota(jnp.int32, (rows, slots), 1) < count[0], on_row, 0.0)
     contract = (((1,), (1,)), ((), ()))
@@ -365,24 +450,102 @@
     lax.fori_loop(0, pairs // group, scatter, 0)
 
 
-def rough_step(bottom, cells, count, targets, n):
+def rough_step(bottom, cells, count, targets, scalars, equil, x, lo, hi, n):
     pairs, rows, width = bottom.shape
     slots = cells.shape[1]
+    half, _, modes, total_rows, _ = x.shape
+    planes = total_rows // rows
+    batch = min(8, modes)
     return pl.pallas_call(
-        functools.partial(rough_kernel, n),
-        out_shape=jax.ShapeDtypeStruct(bottom.shape, F32),
-        in_specs=[whole(pltpu.SMEM), whole(), whole(), whole()],
-        out_specs=whole(),
+        functools.partial(rough_kernel, n, planes),
+        out_shape=(
+            jax.ShapeDtypeStruct(bottom.shape, F32),
+            jax.ShapeDtypeStruct((half, modes, total_rows, width), F32),
+        ),
+        in_specs=[whole(pltpu.SMEM)] * 5 + [whole()] * 4 + [whole(pl.ANY)] * 3,
+        out_specs=(whole(), whole(pl.ANY)),
         scratch_shapes=[
             pltpu.VMEM((n, pairs, slots), F32),
             pltpu.VMEM((pairs, slots), F32),
             pltpu.VMEM((width, slots), BF16),
+            pltpu.VMEM((2, batch, total_rows, width), F32),
+            pltpu.VMEM((2, batch, planes, width), F32),
+            pltpu.VMEM((2, batch, planes, width), F32),
+            pltpu.VMEM((2, batch, total_rows, width), F32),
             pltpu.SemaphoreType.DMA((2, 2, n - 1)),
             pltpu.SemaphoreType.DMA((2, 2, n - 1)),
+            pltpu.SemaphoreType.DMA((4, 2)),
         ],
         compiler_params=pltpu.CompilerParams(collective_id=2, has_side_effects=True),
         name="rough_step",
-    )(count, bottom, cells, targets)
+    )(count, *scalars[:4], bottom, cells, targets, equil, x, lo, hi)
+
+
+def rise_kernel(planes, dir_cos, velocity, rate, weight, base, inflow, before, _, out, energy):
+    h, b = pl.program_id(0), pl.program_id(1)
+    count, total_rows, width = base.shape
+    rows = total_rows // planes
+
+    @pl.when((h == 0) & (b == 0))
+    def _():
+        energy[...] = before[...]
+
+    s = (lax.axis_index("mode") * pl.num_programs(0) + h) * 2
+    cz, w = dir_cos[2, s], weight[s]
+    wide = min(4, count)
+
+    def some(g, carry):
+        picks = [g * wide + t for t in range(wide)]
+        prev_k, values = [], []
+        for i in picks:
+            m = b * count + i
+            turn = velocity[m] * jnp.abs(cz)
+            ratio = jnp.full((rows, width), turn, F32) / jnp.full(
+                (rows, width), 1.0 + rate[m] + turn, F32
+            )
+            prev_k.append(ratio)
+            values.append(inflow[i])
+        for z in range(planes):
+            here = pl.ds(z * rows, rows)
+            total = None
+            for t, i in enumerate(picks):
+                values[t] = prev_k[t] * values[t]
+                value = base[i, here, :] + values[t]
+                out[i, here, :] = value
+                total = value if total is None else total + value
+            energy[here, :] += w * total
+        return carry
+
+    lax.fori_loop(0, count // wide, some, 0)
+
+
+def rise_step(planes, scalars, base, inflow, before, fresh):
+    half, modes, total_rows, width = base.shape
+    rows = total_rows // planes
+    block = min(8, modes)
+    dir_cos, velocity, rate, _, weight = scalars
+    flat = pl.BlockSpec((total_rows, width), lambda h, b: (0, 0))
+    return pl.pallas_call(
+        functools.partial(rise_kernel, planes),
+        grid=(half, modes // block),
+        out_shape=(
+            jax.ShapeDtypeStruct(fresh.shape, F32),
+            jax.ShapeDtypeStruct((total_rows, width), F32),
+        ),
+        in_specs=[whole(pltpu.SMEM)] * 4
+        + [
+            pl.BlockSpec((None, block, total_rows, width), lambda h, b: (h, b, 0, 0)),
+            pl.BlockSpec((None, block, rows, width), lambda h, b: (h, b, 0, 0)),
+            flat,
+            whole(pl.ANY),
+        ],
+        out_specs=(
+            pl.BlockSpec((None, None, block, total_rows, width), lambda h, b: (h, 0, b, 0, 0)),
+            flat,
+        ),
+        input_output_aliases={7: 0},
+        name="rise_step",
+    )(dir_cos, velocity, rate, weight, base, inflow, before, fresh)
 
 
 def sweep_kernel(down, planes, *refs):
@@ -512,13 +675,12 @@
     scalars = (dir_cos, velocity, rate, spectrum, weight)
     fresh, bottom, energy = sweep_step(True, planes, scalars, x, lo, hi, equil, heat)
     targets = lax.dynamic_slice_in_dim(rough_map, position * half, half, 1).T
-    inflow = rough_step(
-        bottom.reshape(half * modes, rows, width), rough_cells[None], rough_count, targets, n
+    inflow, base = rough_step(
+        bottom.reshape(half * modes, rows, width), rough_cells[None], rough_count, targets,
+        scalars, equil, x, lo, hi, n,
     )
     inflow = inflow.reshape(half, modes, rows, width)
-    fresh, energy = sweep_step(
-        False, planes, scalars, x, lo, hi, equil, inflow, energy, fresh
-    )
+    fresh, energy = rise_step(planes, scalars, base, inflow, energy, fresh)
     energy = close_step(energy, n, pairs_total)
     return fresh.reshape(intensity.shape), energy.reshape(planes, rows, width)
 

time: 100 us -> 100 us (level)
    pallas_call x1 -> x2, Pallas kernels: 33.1 us -> 44.6 us  [the longest x1 35.1 us: rough_step(): pl.pallas_call(functools.partial(rough_kernel, n, planes), out_shape=(jax...]
    pallas_call x2 -> x1, Pallas kernels: 23.2 us -> 11.7 us  [sweep_step(): pl.pallas_call(functools.partial(sweep_kernel, down, planes), grid=(half,...]
where the time goes in v3:
time: 100 us; the launch traced here: 99.4 us
  Pallas kernels  95.8 us (96%)
  local copies, waits for them, and re-layouts  2.32 us (2%)
  between operations  1.35 us (1%)
    pallas_call x1, Pallas kernels, rough_step(): pl.pallas_call(functools.partial(rough_kernel, n, planes), out_shape=(jax...  35.1 us
    pallas_call x1, Pallas kernels, open_step(): pl.pallas_call(functools.partial(open_kernel, n, ns, modes, planes, pairs...  26.6 us
    pallas_call x1, Pallas kernels, close_step(): pl.pallas_call(functools.partial(close_kernel, n, pairs_total), out_shape...  12.8 us
    pallas_call x1, Pallas kernels, sweep_step(): pl.pallas_call(functools.partial(sweep_kernel, down, planes), grid=(half,...  11.7 us
    pallas_call x1, Pallas kernels, rise_step(): pl.pallas_call(functools.partial(rise_kernel, planes), grid=(half, modes...  9.54 us

profile of v3, /device:TPU:0, one launch (start us, length us, event | category | flops | bytes accessed | tf_op | source)
XLA Modules:
  0.0 99.4 jit_solution(3139790689584296658)
XLA Ops:
  0.6 0.0 copy-start
  1.3 0.1 copy-done
  1.5 0.6 dynamic-slice_bitcast_fusion.targets
  2.1 26.6 %open_step.1 = (f32[128,256]{1,0:T(8,128)}, f32[128,8,256]{2,1,0:T(8,128)}, f32[128,8,256]{2,1,0:T(8,128)}) custom-call(f32[32]{0:T(128)} %weight.3, f32[128,128,256]{2,1,0:T(8,128)} %bitcast.11), custom_call_target="tpu_custom_call" | custom-call | tf_op jit(solution)/shard_map/open_step/pallas_call | solution.py:211
  28.7 11.7 %down_sweep.1 = (f32[2,2,32,128,256]{4,3,2,1,0:T(8,128)}, f32[2,32,16,256]{3,2,1,0:T(8,128)}, f32[128,256]{1,0:T(8,128)}) custom-call(f32[3,32]{1,0:T(4,128)} %dir_cos.3, f32[32]{0:T(128)} %velocity.3, f32[32]{0:T(128)} %rate.3, f32[32]{0:T(128)} %spectrum.1, f32[32]{0:T(128)} %weight.3, f32[2,2,32,128,256]{4,3,2,1,0:T(8,128)} %bitcast.12, ...), custom_call_target="tpu_custom_call" | custom-call | tf_op jit(solution)/shard_map/down_sweep/pallas_call | solution.py:650
  40.4 35.1 %rough_step.1 = (f32[64,16,256]{2,1,0:T(8,128)}, f32[2,32,128,256]{3,2,1,0:T(8,128)}) custom-call(s32[1]{0:T(128)S(6)} %copy.15.count, f32[3,32]{1,0:T(4,128)} %dir_cos.3, f32[32]{0:T(128)} %velocity.3, f32[32]{0:T(128)} %rate.3, f32[32]{0:T(128)} %spectrum.1, f32[64,16,256]{2,1,0:T(8,128)} %bitcast.20, s32[1,1024]{1,0:T(1,128)} %bitcast.22, ...), custom_call_target="tpu_custom_call" | custom-call | tf_op jit(solution)/shard_map/rough_step/pallas_call | solution.py:459
  75.5 9.5 %rise_step.1 = (f32[2,2,32,128,256]{4,3,2,1,0:T(8,128)}, f32[128,256]{1,0:T(8,128)}) custom-call(f32[3,32]{1,0:T(4,128)} %dir_cos.3, f32[32]{0:T(128)} %velocity.3, f32[32]{0:T(128)} %rate.3, f32[32]{0:T(128)} %weight.3, f32[2,32,128,256]{3,2,1,0:T(8,128)} %get-tuple-element.16.base, f32[2,32,16,256]{3,2,1,0:T(8,128)} %bitcast.19, ...), custom_call_target="tpu_custom_call", output_to_operand_aliasing={{0}: (7, {})} | custom-call | tf_op jit(solution)/shard_map/rise_step/pallas_call | solution.py:528
  85.0 12.8 %close_step.1 = f32[128,256]{1,0:T(8,128)} custom-call(f32[128,256]{1,0:T(8,128)} %get-tuple-element.21.x_ref), custom_call_target="tpu_custom_call" | custom-call | tf_op jit(solution)/shard_map/close_step/pallas_call | solution.py:242
  97.9 1.6 %copy.16 = f32[8,16,256]{2,1,0:T(8,128)} copy(f32[8,16,256]{2,1,0:T(8,128)} %bitcast.21) | data formatting | bytes 262144
Async XLA Ops:
  0.6 0.8 copy-start
